TPU v7x, 32 devices: a whole 2x2x4 slice. The times are simulated.
32 devices in a mesh: dp: 8 (over z, y), layer: 4 (over x, core).
Axes of the slice: x: 2, y: 2, z: 4, core: 2. Of those that a mesh axis runs over, the one named last changes fastest.
Arguments:
- acts: bfloat16 [4, 16, 128, 4096], P('layer', 'dp'), may hold values from -60 to 60
- grads: bfloat16 [4, 16, 128, 14336], P('layer', 'dp'), may hold values from -60 to 60
- proj_in: bfloat16 [4, 64, 4096], P('layer'), may hold values from -0.09375 to 0.09375
- proj_out: bfloat16 [4, 64, 14336], P('layer'), may hold values from -0.046875 to 0.046875
- query_grads: bfloat16 [4, 512, 4096], P('layer', 'dp'), may hold values from -6 to 6
Outputs:
- scores: float32 [16, 512], P('dp', 'layer')
All inputs are finite; a program needn't handle non-finite values.
Results may differ from a plain program's by a relative error of at most 0.004.
Values may be sent and summed in bfloat16 or wider, within the bound.
No kernel may reach another device: no remote copies, remote signals or barrier semaphores. Data moves between devices by JAX's collectives and lax.ppermute only.
A program may use at most 64 MiB of HBM per device.

v0:
```python
import functools
import math

import jax
import jax.numpy as jnp
from jax import lax
from jax.experimental import pallas as pl
from jax.experimental.pallas import tpu as pltpu
from jax.sharding import PartitionSpec as P

HIGHEST = lax.Precision.HIGHEST
ANY = pl.BlockSpec(memory_space=pl.ANY)
VMEM = pl.BlockSpec(memory_space=pltpu.VMEM)
DAMPING = 0.1
PROJECT_VMEM = 16 << 20
SMALL_VMEM = 6 << 20


def dot(a, b, precision=None):
    return jnp.dot(a, b, precision=precision, preferred_element_type=jnp.float32)


def dot_t(a, b, precision=None):
    return lax.dot_general(
        a, b, (((1,), (1,)), ((), ())), precision=precision, preferred_element_type=jnp.float32
    )


def bits(n):
    return [1 << k for k in range(n.bit_length() - 1)]


def chunk_of(width, limit):
    size = min(width, limit)
    while width % size or size % 128:
        size -= 128
    return size


def project_kernel(chunks, acts, grads, p_in, p_out, cov, grad, a_v, g_v, pi_v, po_v, sems):
    examples, length = a_v.shape[0], a_v.shape[1]
    rank = pi_v.shape[0]
    copies = []
    for src, dst, proj, proj_v, size in (
        (acts, a_v, p_in, pi_v, chunks[0]),
        (grads, g_v, p_out, po_v, chunks[1]),
    ):
        for at in range(0, dst.shape[2], size):
            cut = pl.ds(at, size)
            pair = (
                pltpu.make_async_copy(
                    src.at[0, :, :, cut], dst.at[:, :, cut], sems.at[2 * len(copies)]
                ),
                pltpu.make_async_copy(
                    proj.at[0, :, cut], proj_v.at[:, cut], sems.at[2 * len(copies) + 1]
                ),
            )
            for copy in pair:
                copy.start()
            copies.append((pair, dst, proj_v, at, size))
    sums = [None, None]
    for pair, dst, proj_v, at, size in copies:
        for copy in pair:
            copy.wait()
        rows = dst[:, :, at : at + size].reshape(examples * length, size)
        part = dot_t(proj_v[:, at : at + size], rows)
        k = 0 if dst is a_v else 1
        sums[k] = part if sums[k] is None else sums[k] + part
    both = jnp.concatenate([sums[1], sums[0]], axis=0)
    grams = []
    for e in range(examples):
        cut = both[:, e * length : (e + 1) * length]
        grams.append(dot_t(cut, cut, HIGHEST))
    total = functools.reduce(jnp.add, grams)
    low = lax.broadcasted_iota(jnp.int32, (rank, 2 * rank), 1) < rank
    cov[...] = jnp.where(low, total[:rank], total[rank:])
    for k in range(examples // 2):
        first = pltpu.roll(grams[2 * k][:rank], rank, 1)
        grad[k * rank : (k + 1) * rank, :] = jnp.where(low, first, grams[2 * k + 1][:rank])


def project(acts, grads, p_in, p_out):
    _, examples, length, width = acts.shape
    hidden, rank = grads.shape[3], p_in.shape[1]
    chunks = (chunk_of(width, 4096), chunk_of(hidden, 3584))
    count = 2 * (width // chunks[0] + hidden // chunks[1])
    return pl.pallas_call(
        functools.partial(project_kernel, chunks),
        name="project",
        out_shape=(
            jax.ShapeDtypeStruct((rank, 2 * rank), jnp.float32),
            jax.ShapeDtypeStruct((examples // 2 * rank, 2 * rank), jnp.float32),
        ),
        in_specs=[ANY] * 4,
        out_specs=(VMEM, VMEM),
        scratch_shapes=[
            pltpu.VMEM((examples, length, width), acts.dtype),
            pltpu.VMEM((examples, length, hidden), grads.dtype),
            pltpu.VMEM((rank, width), p_in.dtype),
            pltpu.VMEM((rank, hidden), p_out.dtype),
            pltpu.SemaphoreType.DMA((count,)),
        ],
        compiler_params=pltpu.CompilerParams(vmem_limit_bytes=PROJECT_VMEM),
        cost_estimate=pl.CostEstimate(
            flops=2 * examples * length * rank * (width + hidden),
            bytes_accessed=2 * (examples * length + rank) * (width + hidden),
            transcendentals=0,
        ),
    )(*(pltpu.with_memory_space_constraint(x, pltpu.HBM) for x in (acts, grads, p_in, p_out)))


def inverse_plan(rank):
    low = 2 * DAMPING / (rank + 2 * DAMPING)
    scales = []
    while 1 - low > 3e-4:
        prod = low * (2 - low)
        scales.append(2 / (1 + prod))
        low = scales[-1] * prod
    return scales


def inverses(cov):
    rank = cov.shape[0]
    size = 2 * rank
    lane = lax.broadcasted_iota(jnp.int32, (rank, size), 1)
    row = lax.broadcasted_iota(jnp.int32, (rank, size), 0)
    low = lane < rank
    tr_out = jnp.sum(jnp.where(lane == row, cov, 0.0), keepdims=True) / rank
    tr_in = jnp.sum(jnp.where(lane == row + rank, cov, 0.0), keepdims=True) / rank
    big = jnp.concatenate([jnp.where(low, cov, 0.0), jnp.where(low, 0.0, cov)], axis=0)
    eye = (
        lax.broadcasted_iota(jnp.int32, (size, size), 0)
        == lax.broadcasted_iota(jnp.int32, (size, size), 1)
    ).astype(jnp.float32)
    upper = lax.broadcasted_iota(jnp.int32, (size, 1), 0) < rank
    mean = jnp.where(upper, tr_out, tr_in)
    factor = big + (DAMPING * mean) * eye
    start = 2.0 / ((rank + 2 * DAMPING) * mean)
    m = factor * start
    x = None
    scales = inverse_plan(rank)
    for k, c in enumerate(scales):
        q = (2 * c) * eye - c * m
        if x is None:
            x = q
            m = dot(m, q, HIGHEST)
        elif k < len(scales) - 1:
            both = dot(jnp.concatenate([x, m], axis=0), q, HIGHEST)
            x, m = both[:size], both[size:]
        else:
            x = dot(x, q, HIGHEST)
    x = x * start
    rest = eye - dot(factor, x, HIGHEST)
    return x + dot(x, rest, HIGHEST)


def inverse_kernel(tokens, cov_a, cov_b, out):
    out[...] = inverses(cov_a[...] + cov_b[...]) * tokens


def inverses_of(tokens, cov_a, cov_b):
    size = cov_a.shape[1]
    return pl.pallas_call(
        functools.partial(inverse_kernel, float(tokens)),
        name="inverses",
        out_shape=jax.ShapeDtypeStruct((size, size), jnp.float32),
        in_specs=[VMEM] * 2,
        out_specs=VMEM,
        compiler_params=pltpu.CompilerParams(vmem_limit_bytes=SMALL_VMEM),
        cost_estimate=pl.CostEstimate(
            flops=200 * size**3, bytes_accessed=16 * size * size, transcendentals=0
        ),
    )(cov_a, cov_b)


def score_kernel(r, scale, inv, *refs):
    queries, (*grads, out, cond_s, q_v, sems) = refs[:r], refs[r:]
    size = inv.shape[1]
    rank = size // 2
    count = queries[0].shape[0]
    mine = lax.rem(lax.axis_index("dp"), r)
    copies = []
    for k in range(r):
        at = pl.multiple_of((mine ^ k) * count, count)
        copy = pltpu.make_async_copy(queries[k], q_v.at[pl.ds(at, count)], sems.at[k])
        copy.start()
        copies.append(copy)
    f_out = inv[:rank, :rank]
    f_in = inv[rank:, :]
    twice_in = jnp.concatenate([pltpu.roll(f_in, rank, 1), f_in], axis=0)
    pieces = [g[at : at + rank, :] for g in grads for at in range(0, g.shape[0], rank)]
    blocks = len(pieces)
    left = dot(f_out, jnp.concatenate(pieces, axis=1), HIGHEST)
    left = jnp.concatenate([left[:, size * k : size * (k + 1)] for k in range(blocks)], axis=0)
    cond = dot(left, twice_in, HIGHEST)
    n = blocks * rank
    cond_s[0:n, :] = cond
    cond_s[n : 2 * n, :] = pltpu.roll(cond, rank, 1)
    cond_s[2 * n :, :] = cond
    low = lax.broadcasted_iota(jnp.int32, (2 * blocks, size), 1) < rank
    parts = []
    for j in range(rank // 2):
        even = cond_s[pl.ds(2 * j, 2 * blocks, stride=rank), :]
        odd = cond_s[pl.ds(n + 2 * j + 1, 2 * blocks, stride=rank), :]
        parts.append(jnp.where(low, even, odd))
    flat = jnp.concatenate(parts, axis=1).astype(jnp.bfloat16)
    for copy in copies:
        copy.wait()
    out[...] = dot_t(flat, q_v[...]) * scale


def scores_of(r, scale, inv, queries, grads):
    size = inv.shape[1]
    blocks = sum(g.shape[0] for g in grads) // (size // 2)
    count, width = queries[0].shape
    return pl.pallas_call(
        functools.partial(score_kernel, r, scale),
        name="scores",
        out_shape=jax.ShapeDtypeStruct((2 * blocks, r * count), jnp.float32),
        in_specs=[VMEM] + [ANY] * r + [VMEM] * len(grads),
        out_specs=VMEM,
        scratch_shapes=[
            pltpu.VMEM((3 * blocks * (size // 2), size), jnp.float32),
            pltpu.VMEM((r * count, width), queries[0].dtype),
            pltpu.SemaphoreType.DMA((r,)),
        ],
        compiler_params=pltpu.CompilerParams(vmem_limit_bytes=SMALL_VMEM),
        cost_estimate=pl.CostEstimate(
            flops=4 * blocks * r * count * width,
            bytes_accessed=2 * r * count * width,
            transcendentals=0,
        ),
    )(inv, *queries, *grads)


def local(n_dp, n_layer, acts, grads, proj_in, proj_out, query_grads):
    _, examples, length = acts.shape[:3]
    r = n_dp // n_layer
    assert acts.shape[0] == 1 and examples == 2 and r * n_layer == n_dp

    def swap(x, axis, n, k):
        return lax.ppermute(x, axis, [(i, i ^ k) for i in range(n)])

    cov, grad = project(acts, grads, proj_in, proj_out)
    steps = bits(r) + [r * k for k in bits(n_layer)]
    queries = [query_grads[0]]
    for k in range(1, r):
        queries.append(swap(query_grads[0], "dp", n_dp, k))
    gathered = [grad]
    for s, k in enumerate(steps):
        other = swap(cov, "dp", n_dp, k)
        if k >= r:
            whole = jnp.concatenate(gathered, axis=0) if len(gathered) > 1 else gathered[0]
            gathered.append(swap(whole, "dp", n_dp, k))
        if s < len(steps) - 1:
            cov = cov + other
    width = query_grads.shape[2]
    scale = 1.0 / math.sqrt(width * acts.shape[0] * n_layer * length)
    inv = inverses_of(examples * length * n_dp, cov, other)
    part = scores_of(r, scale, inv, queries, gathered)
    for k in bits(n_layer):
        part = part + swap(part, "layer", n_layer, k)
    pick = (lax.axis_index("dp") // r) ^ lax.axis_index("layer")
    part = lax.dynamic_slice_in_dim(part.reshape(examples, n_layer, -1), pick, 1, axis=1)[:, 0]
    moves = []
    for a in range(n_layer):
        for b in range(r):
            for m in range(n_layer):
                moves.append(((a * r + b) * n_layer + m, (m * r + b) * n_layer + a))
    return lax.ppermute(part, ("dp", "layer"), moves)


def solution(mesh):
    n_dp, n_layer = mesh.shape["dp"], mesh.shape["layer"]

    def body(*args):
        return local(n_dp, n_layer, *args)

    return jax.shard_map(
        body,
        mesh=mesh,
        in_specs=(
            P("layer", "dp", None, None),
            P("layer", "dp", None, None),
            P("layer", None, None),
            P("layer", None, None),
            P("layer", "dp", None),
        ),
        out_specs=P("dp", "layer"),
        check_vma=False,
    )
```

profile of v0, /device:TPU:24, one launch (start us, length us, event | category | flops | bytes accessed | tf_op | source)
XLA Modules:
  0.0 40.6 jit_solution(15325572021350155387)
XLA Ops:
  0.0 1.5 %collective-permute-start.3 = (bf16[64,4096]{1,0:T(8,128)(2,1)}, bf16[64,4096]{1,0:T(8,128)(2,1)S(1)}, u32[]{:S(2)}, u32[]{:S(2)}) collective-permute-start(bf16[64,4096]{1,0:T(8,128)(2,1)} %bitcast.3), channel_id=1, source_target_pairs={{0,4},{4,0},{8,12},{12,8},{16,20},{20,16},{24,28},{28,24},{1,5},{5... | collective-permute-start | bytes 1572872 | tf_op jit(solution)/shard_map/ppermute | solution.py:242
  1.5 7.1 %project.1 = (f32[64,128]{1,0:T(8,128)S(1)}, f32[64,128]{1,0:T(8,128)S(1)}) custom-call(bf16[1,2,128,4096]{3,2,1,0:T(8,128)(2,1)} %acts.1, bf16[1,2,128,14336]{3,2,1,0:T(8,128)(2,1)} %grads.1, bf16[1,64,4096]{2,1,0:T(8,128)(2,1)} %p_in.1, bf16[1,64,14336]{2,1,0:T(8,128)(2,1)} %p_out.1), custom_call_target="tpu_custom_call" | custom-call | flops 603979776 | bytes 11796480 | tf_op jit(solution)/shard_map/project/pallas_call | solution.py:87
  8.6 0.0 copy-start
  8.6 0.6 %collective-permute-start = (f32[64,128]{1,0:T(8,128)S(1)}, f32[64,128]{1,0:T(8,128)S(1)}, u32[]{:S(2)}, u32[]{:S(2)}) collective-permute-start(f32[64,128]{1,0:T(8,128)S(1)} %get-tuple-element.7), channel_id=1, source_target_pairs={{0,4},{4,0},{8,12},{12,8},{16,20},{20,16},{24,28},{28,24},{1,5},{5... | collective-permute-start | bytes 98312 | tf_op jit(solution)/shard_map/ppermute | solution.py:242
  9.2 5.4 %collective-permute-done = f32[64,128]{1,0:T(8,128)S(1)} collective-permute-done((f32[64,128]{1,0:T(8,128)S(1)}, f32[64,128]{1,0:T(8,128)S(1)}, u32[]{:S(2)}, u32[]{:S(2)}) %collective-permute-start) | collective-permute-done | bytes 32800 | tf_op jit(solution)/shard_map/ppermute | solution.py:242
  14.6 0.4 %collective-permute-start.1 = (f32[64,128]{1,0:T(8,128)S(1)}, f32[64,128]{1,0:T(8,128)S(1)}, u32[]{:S(2)}, u32[]{:S(2)}) collective-permute-start(f32[64,128]{1,0:T(8,128)S(1)} %add.16), channel_id=1, source_target_pairs={{0,8},{4,12},{8,0},{12,4},{16,24},{20,28},{24,16},{28,20},{1,9},{5... | collective-permute-start | bytes 98312 | tf_op jit(solution)/shard_map/ppermute | solution.py:242
  15.0 1.6 %collective-permute-start.4 = (f32[64,128]{1,0:T(8,128)S(1)}, f32[64,128]{1,0:T(8,128)S(1)}, u32[]{:S(2)}, u32[]{:S(2)}) collective-permute-start(f32[64,128]{1,0:T(8,128)S(1)} %get-tuple-element.8.refs_2_), channel_id=1, source_target_pairs={{0,8},{4,12},{8,0},{12,4},{16,24},{20,28},{24,16},{28,20},{1,9},{5... | collective-permute-start | bytes 98312 | tf_op jit(solution)/shard_map/ppermute | solution.py:242
  16.6 1.9 %collective-permute-done.1 = f32[64,128]{1,0:T(8,128)S(1)} collective-permute-done((f32[64,128]{1,0:T(8,128)S(1)}, f32[64,128]{1,0:T(8,128)S(1)}, u32[]{:S(2)}, u32[]{:S(2)}) %collective-permute-start.1) | collective-permute-done | bytes 32800 | tf_op jit(solution)/shard_map/ppermute | solution.py:242
  18.5 0.3 collective-permute-start.2
  18.8 0.1 collective-permute-done.4.refs_3_
  19.0 2.6 %collective-permute-start.5 = (f32[128,128]{1,0:T(8,128)S(1)}, f32[128,128]{1,0:T(8,128)S(1)}, u32[]{:S(2)}, u32[]{:S(2)}) collective-permute-start(f32[128,128]{1,0:T(8,128)S(1)} %pad_maximum_fusion), channel_id=1, source_target_pairs={{0,16},{4,20},{8,24},{12,28},{16,0},{20,4},{24,8},{28,12},{1,17},{... | collective-permute-start | bytes 196616 | tf_op jit(solution)/shard_map/ppermute | solution.py:242
  21.5 2.0 %collective-permute-done.2.cov_b = f32[64,128]{1,0:T(8,128)S(1)} collective-permute-done((f32[64,128]{1,0:T(8,128)S(1)}, f32[64,128]{1,0:T(8,128)S(1)}, u32[]{:S(2)}, u32[]{:S(2)}) %collective-permute-start.2) | collective-permute-done | bytes 32800 | tf_op jit(solution)/shard_map/ppermute | solution.py:242
  23.6 2.6 %inverses.1.inv = f32[128,128]{1,0:T(8,128)S(1)} custom-call(f32[64,128]{1,0:T(8,128)S(1)} %add.17.cov_a, f32[64,128]{1,0:T(8,128)S(1)} %collective-permute-done.2.cov_b), custom_call_target="tpu_custom_call" | custom-call | flops 419430400 | bytes 262144 | tf_op jit(solution)/shard_map/inverses/pallas_call | solution.py:163
  26.2 0.0 collective-permute-done.5.refs_4_
  26.2 0.0 collective-permute-done.3.refs_1_
  26.2 0.0 copy-done
  26.2 1.4 %scores.1 = f32[8,128]{1,0:T(8,128)S(1)} custom-call(f32[128,128]{1,0:T(8,128)S(1)} %inverses.1.inv, bf16[64,4096]{1,0:T(8,128)(2,1)S(1)} %bitcast.4, bf16[64,4096]{1,0:T(8,128)(2,1)S(1)} %collective-permute-done.3.refs_1_, f32[64,128]{1,0:T(8,128)S(1)} %get-tuple-element.8.refs_2_, f32[64,128]{1,0:T(8,128)S(1)} %collective-permute-done.4.refs_3_, ...), custom_call_target="tpu_custom_call" | custom-call | flops 8388608 | bytes 1048576 | tf_op jit(solution)/shard_map/scores/pallas_call | solution.py:216
  27.6 0.1 collective-permute-start.6
  27.7 1.2 %collective-permute-done.6 = f32[8,128]{1,0:T(8,128)S(1)} collective-permute-done((f32[8,128]{1,0:T(8,128)S(1)}, f32[8,128]{1,0:T(8,128)S(1)}, u32[]{:S(2)}, u32[]{:S(2)}) %collective-permute-start.6) | collective-permute-done | bytes 4128 | tf_op jit(solution)/shard_map/ppermute | solution.py:242
  28.9 1.5 %collective-permute-start.7 = (f32[8,128]{1,0:T(8,128)S(1)}, f32[8,128]{1,0:T(8,128)S(1)}, u32[]{:S(2)}, u32[]{:S(2)}) collective-permute-start(f32[8,128]{1,0:T(8,128)S(1)} %add.18), channel_id=1, source_target_pairs={{0,2},{1,3},{2,0},{3,1},{4,6},{5,7},{6,4},{7,5},{8,10},{9,11},{10,... | collective-permute-start | bytes 12296 | tf_op jit(solution)/shard_map/ppermute | solution.py:242
  30.4 2.1 %collective-permute-done.7 = f32[8,128]{1,0:T(8,128)S(1)} collective-permute-done((f32[8,128]{1,0:T(8,128)S(1)}, f32[8,128]{1,0:T(8,128)S(1)}, u32[]{:S(2)}, u32[]{:S(2)}) %collective-permute-start.7) | collective-permute-done | bytes 4128 | tf_op jit(solution)/shard_map/ppermute | solution.py:242
  32.5 1.9 %collective-permute-start.8 = (f32[2,128]{1,0:T(2,128)S(1)}, f32[2,128]{1,0:T(2,128)S(1)}, u32[]{:S(2)}, u32[]{:S(2)}) collective-permute-start(f32[2,128]{1,0:T(2,128)S(1)} %bitcast.6), channel_id=1, source_target_pairs={{0,0},{1,8},{2,16},{3,24},{4,4},{5,12},{6,20},{7,28},{8,1},{9,9},{... | collective-permute-start | bytes 3080 | tf_op jit(solution)/shard_map/ppermute | solution.py:270
  34.4 5.7 %collective-permute-done.8 = f32[2,128]{1,0:T(2,128)S(1)} collective-permute-done((f32[2,128]{1,0:T(2,128)S(1)}, f32[2,128]{1,0:T(2,128)S(1)}, u32[]{:S(2)}, u32[]{:S(2)}) %collective-permute-start.8) | collective-permute-done | bytes 1056 | tf_op jit(solution)/shard_map/ppermute | solution.py:270
  40.1 0.6 %copy.7 = f32[2,128]{1,0:T(2,128)} copy(f32[2,128]{1,0:T(2,128)S(1)} %collective-permute-done.8) | data formatting | bytes 2048
  (6 shorter events, 0.0 us)
Async XLA Ops:
  0.0 26.2 %collective-permute-start.3 = (bf16[64,4096]{1,0:T(8,128)(2,1)}, bf16[64,4096]{1,0:T(8,128)(2,1)S(1)}, u32[]{:S(2)}, u32[]{:S(2)}) collective-permute-start(bf16[64,4096]{1,0:T(8,128)(2,1)} %bitcast.3), channel_id=1, source_target_pairs={{0,4},{4,0},{8,12},{12,8},{16,20},{20,16},{24,28},{28,24},{1,5},{5... | collective-permute-start | bytes 1572872 | tf_op jit(solution)/shard_map/ppermute | solution.py:242
  8.6 17.6 %copy-start = (bf16[1,64,4096]{2,1,0:T(8,128)(2,1)S(1)}, bf16[1,64,4096]{2,1,0:T(8,128)(2,1)}, u32[]{:S(2)}) copy-start(bf16[1,64,4096]{2,1,0:T(8,128)(2,1)} %param.9) | copy-start | bytes 1572868
  8.6 6.0 %collective-permute-start = (f32[64,128]{1,0:T(8,128)S(1)}, f32[64,128]{1,0:T(8,128)S(1)}, u32[]{:S(2)}, u32[]{:S(2)}) collective-permute-start(f32[64,128]{1,0:T(8,128)S(1)} %get-tuple-element.7), channel_id=1, source_target_pairs={{0,4},{4,0},{8,12},{12,8},{16,20},{20,16},{24,28},{28,24},{1,5},{5... | collective-permute-start | bytes 98312 | tf_op jit(solution)/shard_map/ppermute | solution.py:242
  14.6 3.9 %collective-permute-start.1 = (f32[64,128]{1,0:T(8,128)S(1)}, f32[64,128]{1,0:T(8,128)S(1)}, u32[]{:S(2)}, u32[]{:S(2)}) collective-permute-start(f32[64,128]{1,0:T(8,128)S(1)} %add.16), channel_id=1, source_target_pairs={{0,8},{4,12},{8,0},{12,4},{16,24},{20,28},{24,16},{28,20},{1,9},{5... | collective-permute-start | bytes 98312 | tf_op jit(solution)/shard_map/ppermute | solution.py:242
  15.0 3.9 %collective-permute-start.4 = (f32[64,128]{1,0:T(8,128)S(1)}, f32[64,128]{1,0:T(8,128)S(1)}, u32[]{:S(2)}, u32[]{:S(2)}) collective-permute-start(f32[64,128]{1,0:T(8,128)S(1)} %get-tuple-element.8.refs_2_), channel_id=1, source_target_pairs={{0,8},{4,12},{8,0},{12,4},{16,24},{20,28},{24,16},{28,20},{1,9},{5... | collective-permute-start | bytes 98312 | tf_op jit(solution)/shard_map/ppermute | solution.py:242
  18.5 5.1 %collective-permute-start.2 = (f32[64,128]{1,0:T(8,128)S(1)}, f32[64,128]{1,0:T(8,128)S(1)}, u32[]{:S(2)}, u32[]{:S(2)}) collective-permute-start(f32[64,128]{1,0:T(8,128)S(1)} %add.17.cov_a), channel_id=1, source_target_pairs={{0,16},{4,20},{8,24},{12,28},{16,0},{20,4},{24,8},{28,12},{1,17},{... | collective-permute-start | bytes 98312 | tf_op jit(solution)/shard_map/ppermute | solution.py:242
  19.0 7.3 %collective-permute-start.5 = (f32[128,128]{1,0:T(8,128)S(1)}, f32[128,128]{1,0:T(8,128)S(1)}, u32[]{:S(2)}, u32[]{:S(2)}) collective-permute-start(f32[128,128]{1,0:T(8,128)S(1)} %pad_maximum_fusion), channel_id=1, source_target_pairs={{0,16},{4,20},{8,24},{12,28},{16,0},{20,4},{24,8},{28,12},{1,17},{... | collective-permute-start | bytes 196616 | tf_op jit(solution)/shard_map/ppermute | solution.py:242
  27.6 1.2 %collective-permute-start.6 = (f32[8,128]{1,0:T(8,128)S(1)}, f32[8,128]{1,0:T(8,128)S(1)}, u32[]{:S(2)}, u32[]{:S(2)}) collective-permute-start(f32[8,128]{1,0:T(8,128)S(1)} %scores.1), channel_id=1, source_target_pairs={{0,1},{1,0},{2,3},{3,2},{4,5},{5,4},{6,7},{7,6},{8,9},{9,8},{10,11... | collective-permute-start | bytes 12296 | tf_op jit(solution)/shard_map/ppermute | solution.py:242
  28.9 3.6 %collective-permute-start.7 = (f32[8,128]{1,0:T(8,128)S(1)}, f32[8,128]{1,0:T(8,128)S(1)}, u32[]{:S(2)}, u32[]{:S(2)}) collective-permute-start(f32[8,128]{1,0:T(8,128)S(1)} %add.18), channel_id=1, source_target_pairs={{0,2},{1,3},{2,0},{3,1},{4,6},{5,7},{6,4},{7,5},{8,10},{9,11},{10,... | collective-permute-start | bytes 12296 | tf_op jit(solution)/shard_map/ppermute | solution.py:242
  32.5 7.6 %collective-permute-start.8 = (f32[2,128]{1,0:T(2,128)S(1)}, f32[2,128]{1,0:T(2,128)S(1)}, u32[]{:S(2)}, u32[]{:S(2)}) collective-permute-start(f32[2,128]{1,0:T(2,128)S(1)} %bitcast.6), channel_id=1, source_target_pairs={{0,0},{1,8},{2,16},{3,24},{4,4},{5,12},{6,20},{7,28},{8,1},{9,9},{... | collective-permute-start | bytes 3080 | tf_op jit(solution)/shard_map/ppermute | solution.py:270
where the time goes:
time: 40.8 us; the launch traced here: 40.6 us
  waiting for transfers between devices  18.4 us (45%)
  Pallas kernels  11.1 us (27%)
  starting transfers between devices  10.5 us (26%)
  local copies, waits for them, and re-layouts  0.58 us (1%)
    ppermute x8, waiting for transfers between devices, swap(): return lax.ppermute(x, axis, [(i, i ^ k) for i in range(n)])  12.7 us
    ppermute x8, starting transfers between devices, swap(): return lax.ppermute(x, axis, [(i, i ^ k) for i in range(n)])  8.57 us
    pallas_call x1, Pallas kernels, project(): pl.pallas_call(functools.partial(project_kernel, chunks), name='project',...  7.07 us
    ppermute x1, waiting for transfers between devices, local(): return lax.ppermute(part, ('dp', 'layer'), moves)  5.66 us
    pallas_call x1, Pallas kernels, inverses_of(): pl.pallas_call(functools.partial(inverse_kernel, float(tokens)), name='in...  2.64 us
    ppermute x1, starting transfers between devices, local(): return lax.ppermute(part, ('dp', 'layer'), moves)  1.92 us
    pallas_call x1, Pallas kernels, scores_of(): pl.pallas_call(functools.partial(score_kernel, r, scale), name='scores',...  1.39 us
  transfers between devices with their start and end apart: 9, of which 7 were waited for; matrix products, arithmetic and copies ran while one was open for 0% of the time, Pallas kernels for 24%

commit v1 on v0

--- a/solution.py
+++ b/solution.py
@@ -37,35 +37,42 @@
     return size
 
 
-def project_kernel(chunks, acts, grads, p_in, p_out, cov, grad, a_v, g_v, pi_v, po_v, sems):
+def project_kernel(chunks, depth, acts, grads, p_in, p_out, cov, grad, *scratch):
+    a_v, g_v, pi_v, po_v, sums, sems = scratch
     examples, length = a_v.shape[0], a_v.shape[1]
     rank = pi_v.shape[0]
-    copies = []
-    for src, dst, proj, proj_v, size in (
-        (acts, a_v, p_in, pi_v, chunks[0]),
-        (grads, g_v, p_out, po_v, chunks[1]),
+    always = lax.axis_index("dp") >= 0
+    loads = []
+    for k, (src, dst, proj, proj_v) in enumerate(
+        ((acts, a_v, p_in, pi_v), (grads, g_v, p_out, po_v))
     ):
-        for at in range(0, dst.shape[2], size):
-            cut = pl.ds(at, size)
+        for at in range(0, dst.shape[2], chunks[k]):
+            cut = pl.ds(at, chunks[k])
+            sem = 2 * len(loads)
             pair = (
-                pltpu.make_async_copy(
-                    src.at[0, :, :, cut], dst.at[:, :, cut], sems.at[2 * len(copies)]
-                ),
-                pltpu.make_async_copy(
-                    proj.at[0, :, cut], proj_v.at[:, cut], sems.at[2 * len(copies) + 1]
-                ),
+                pltpu.make_async_copy(src.at[0, :, :, cut], dst.at[:, :, cut], sems.at[sem]),
+                pltpu.make_async_copy(proj.at[0, :, cut], proj_v.at[:, cut], sems.at[sem + 1]),
             )
-            for copy in pair:
+            loads.append((pair, k, dst, proj_v, at))
+
+    def start(i):
+        if i < len(loads):
+            for copy in loads[i][0]:
                 copy.start()
-            copies.append((pair, dst, proj_v, at, size))
-    sums = [None, None]
-    for pair, dst, proj_v, at, size in copies:
+
+    for i in range(depth):
+        start(i)
+    for i, (pair, k, dst, proj_v, at) in enumerate(loads):
         for copy in pair:
             copy.wait()
-        rows = dst[:, :, at : at + size].reshape(examples * length, size)
-        part = dot_t(proj_v[:, at : at + size], rows)
-        k = 0 if dst is a_v else 1
-        sums[k] = part if sums[k] is None else sums[k] + part
+        start(i + depth)
+
+        @pl.when(always)
+        def _():
+            rows = dst[:, :, at : at + chunks[k]].reshape(examples * length, chunks[k])
+            part = dot_t(proj_v[:, at : at + chunks[k]], rows)
+            sums[k] = part if at == 0 else sums[k] + part
+
     both = jnp.concatenate([sums[1], sums[0]], axis=0)
     grams = []
     for e in range(examples):
@@ -82,10 +89,10 @@
 def project(acts, grads, p_in, p_out):
     _, examples, length, width = acts.shape
     hidden, rank = grads.shape[3], p_in.shape[1]
-    chunks = (chunk_of(width, 4096), chunk_of(hidden, 3584))
+    chunks = (chunk_of(width, 2048), chunk_of(hidden, 2048))
     count = 2 * (width // chunks[0] + hidden // chunks[1])
     return pl.pallas_call(
-        functools.partial(project_kernel, chunks),
+        functools.partial(project_kernel, chunks, 4),
         name="project",
         out_shape=(
             jax.ShapeDtypeStruct((rank, 2 * rank), jnp.float32),
@@ -98,6 +105,7 @@
             pltpu.VMEM((examples, length, hidden), grads.dtype),
             pltpu.VMEM((rank, width), p_in.dtype),
             pltpu.VMEM((rank, hidden), p_out.dtype),
+            pltpu.VMEM((2, rank, examples * length), jnp.float32),
             pltpu.SemaphoreType.DMA((count,)),
         ],
         compiler_params=pltpu.CompilerParams(vmem_limit_bytes=PROJECT_VMEM),
@@ -260,13 +268,14 @@
     part = scores_of(r, scale, inv, queries, gathered)
     for k in bits(n_layer):
         part = part + swap(part, "layer", n_layer, k)
-    pick = (lax.axis_index("dp") // r) ^ lax.axis_index("layer")
+    half = n_layer // 2
+    pick = (lax.axis_index("dp") // r) ^ lax.axis_index("layer") ^ half
     part = lax.dynamic_slice_in_dim(part.reshape(examples, n_layer, -1), pick, 1, axis=1)[:, 0]
     moves = []
     for a in range(n_layer):
         for b in range(r):
             for m in range(n_layer):
-                moves.append(((a * r + b) * n_layer + m, (m * r + b) * n_layer + a))
+                moves.append(((a * r + b) * n_layer + m, ((m ^ half) * r + b) * n_layer + a))
     return lax.ppermute(part, ("dp", "layer"), moves)
 
 

time: 40.8 us -> 38.7 us (0.949)
  the two profiles are of different devices: /device:TPU:24 before, /device:TPU:0 now
where the time goes in v1:
time: 38.7 us; the launch traced here: 38.3 us
  waiting for transfers between devices  14.3 us (37%)
  starting transfers between devices  13.4 us (35%)
  Pallas kernels  9.93 us (26%)
  local copies, waits for them, and re-layouts  0.58 us (1%)
    ppermute x8, waiting for transfers between devices, swap(): return lax.ppermute(x, axis, [(i, i ^ k) for i in range(n)])  13 us
    ppermute x8, starting transfers between devices, swap(): return lax.ppermute(x, axis, [(i, i ^ k) for i in range(n)])  11 us
    pallas_call x1, Pallas kernels, project(): pl.pallas_call(functools.partial(project_kernel, chunks, 4), name='projec...  5.92 us
    pallas_call x1, Pallas kernels, inverses_of(): pl.pallas_call(functools.partial(inverse_kernel, float(tokens)), name='in...  2.64 us
    ppermute x1, starting transfers between devices, local(): return lax.ppermute(part, ('dp', 'layer'), moves)  2.34 us
    pallas_call x1, Pallas kernels, scores_of(): pl.pallas_call(functools.partial(score_kernel, r, scale), name='scores',...  1.37 us
    ppermute x1, waiting for transfers between devices, local(): return lax.ppermute(part, ('dp', 'layer'), moves)  1.3 us
  transfers between devices with their start and end apart: 9, of which 7 were waited for; matrix products, arithmetic and copies ran while one was open for 0% of the time, Pallas kernels for 22%

profile of v1, /device:TPU:0, one launch (start us, length us, event | category | flops | bytes accessed | tf_op | source)
XLA Modules:
  0.0 38.3 jit_solution(15996430452002399896)
XLA Ops:
  0.0 3.0 %collective-permute-start.3 = (bf16[64,4096]{1,0:T(8,128)(2,1)}, bf16[64,4096]{1,0:T(8,128)(2,1)S(1)}, u32[]{:S(2)}, u32[]{:S(2)}) collective-permute-start(bf16[64,4096]{1,0:T(8,128)(2,1)} %bitcast.3), channel_id=1, source_target_pairs={{0,4},{4,0},{8,12},{12,8},{16,20},{20,16},{24,28},{28,24},{1,5},{5... | collective-permute-start | bytes 1572872 | tf_op jit(solution)/shard_map/ppermute | solution.py:250
  3.0 5.9 %project.1 = (f32[64,128]{1,0:T(8,128)S(1)}, f32[64,128]{1,0:T(8,128)S(1)}) custom-call(bf16[1,2,128,4096]{3,2,1,0:T(8,128)(2,1)} %acts.1, bf16[1,2,128,14336]{3,2,1,0:T(8,128)(2,1)} %grads.1, bf16[1,64,4096]{2,1,0:T(8,128)(2,1)} %p_in.1, bf16[1,64,14336]{2,1,0:T(8,128)(2,1)} %p_out.1), custom_call_target="tpu_custom_call" | custom-call | flops 603979776 | bytes 11796480 | tf_op jit(solution)/shard_map/project/pallas_call | solution.py:94
  8.9 0.0 copy-start
  8.9 0.1 collective-permute-start
  9.0 6.8 %collective-permute-done = f32[64,128]{1,0:T(8,128)S(1)} collective-permute-done((f32[64,128]{1,0:T(8,128)S(1)}, f32[64,128]{1,0:T(8,128)S(1)}, u32[]{:S(2)}, u32[]{:S(2)}) %collective-permute-start) | collective-permute-done | bytes 32800 | tf_op jit(solution)/shard_map/ppermute | solution.py:250
  15.8 1.8 %collective-permute-start.1 = (f32[64,128]{1,0:T(8,128)S(1)}, f32[64,128]{1,0:T(8,128)S(1)}, u32[]{:S(2)}, u32[]{:S(2)}) collective-permute-start(f32[64,128]{1,0:T(8,128)S(1)} %add.16), channel_id=1, source_target_pairs={{0,8},{4,12},{8,0},{12,4},{16,24},{20,28},{24,16},{28,20},{1,9},{5... | collective-permute-start | bytes 98312 | tf_op jit(solution)/shard_map/ppermute | solution.py:250
  17.6 0.2 collective-permute-start.4
  17.9 1.9 %collective-permute-done.1 = f32[64,128]{1,0:T(8,128)S(1)} collective-permute-done((f32[64,128]{1,0:T(8,128)S(1)}, f32[64,128]{1,0:T(8,128)S(1)}, u32[]{:S(2)}, u32[]{:S(2)}) %collective-permute-start.1) | collective-permute-done | bytes 32800 | tf_op jit(solution)/shard_map/ppermute | solution.py:250
  19.8 2.8 %collective-permute-start.2 = (f32[64,128]{1,0:T(8,128)S(1)}, f32[64,128]{1,0:T(8,128)S(1)}, u32[]{:S(2)}, u32[]{:S(2)}) collective-permute-start(f32[64,128]{1,0:T(8,128)S(1)} %add.17.cov_a), channel_id=1, source_target_pairs={{0,16},{4,20},{8,24},{12,28},{16,0},{20,4},{24,8},{28,12},{1,17},{... | collective-permute-start | bytes 98312 | tf_op jit(solution)/shard_map/ppermute | solution.py:250
  22.6 0.0 collective-permute-done.4.refs_3_
  22.6 1.6 %collective-permute-start.5 = (f32[128,128]{1,0:T(8,128)S(1)}, f32[128,128]{1,0:T(8,128)S(1)}, u32[]{:S(2)}, u32[]{:S(2)}) collective-permute-start(f32[128,128]{1,0:T(8,128)S(1)} %pad_maximum_fusion), channel_id=1, source_target_pairs={{0,16},{4,20},{8,24},{12,28},{16,0},{20,4},{24,8},{28,12},{1,17},{... | collective-permute-start | bytes 196616 | tf_op jit(solution)/shard_map/ppermute | solution.py:250
  24.1 0.6 %collective-permute-done.2.cov_b = f32[64,128]{1,0:T(8,128)S(1)} collective-permute-done((f32[64,128]{1,0:T(8,128)S(1)}, f32[64,128]{1,0:T(8,128)S(1)}, u32[]{:S(2)}, u32[]{:S(2)}) %collective-permute-start.2) | collective-permute-done | bytes 32800 | tf_op jit(solution)/shard_map/ppermute | solution.py:250
  24.8 2.6 %inverses.1.inv = f32[128,128]{1,0:T(8,128)S(1)} custom-call(f32[64,128]{1,0:T(8,128)S(1)} %add.17.cov_a, f32[64,128]{1,0:T(8,128)S(1)} %collective-permute-done.2.cov_b), custom_call_target="tpu_custom_call" | custom-call | flops 419430400 | bytes 262144 | tf_op jit(solution)/shard_map/inverses/pallas_call | solution.py:171
  27.4 0.4 %collective-permute-done.5.refs_4_ = f32[128,128]{1,0:T(8,128)S(1)} collective-permute-done((f32[128,128]{1,0:T(8,128)S(1)}, f32[128,128]{1,0:T(8,128)S(1)}, u32[]{:S(2)}, u32[]{:S(2)}) %collective-permute-start.5) | collective-permute-done | bytes 65568 | tf_op jit(solution)/shard_map/ppermute | solution.py:250
  27.8 0.0 collective-permute-done.3.refs_1_
  27.8 0.0 copy-done
  27.8 1.4 %scores.1 = f32[8,128]{1,0:T(8,128)S(1)} custom-call(f32[128,128]{1,0:T(8,128)S(1)} %inverses.1.inv, bf16[64,4096]{1,0:T(8,128)(2,1)S(1)} %bitcast.4, bf16[64,4096]{1,0:T(8,128)(2,1)S(1)} %collective-permute-done.3.refs_1_, f32[64,128]{1,0:T(8,128)S(1)} %get-tuple-element.8.refs_2_, f32[64,128]{1,0:T(8,128)S(1)} %collective-permute-done.4.refs_3_, ...), custom_call_target="tpu_custom_call" | custom-call | flops 8388608 | bytes 1048576 | tf_op jit(solution)/shard_map/scores/pallas_call | solution.py:224
  29.2 0.1 collective-permute-start.6
  29.3 1.2 %collective-permute-done.6 = f32[8,128]{1,0:T(8,128)S(1)} collective-permute-done((f32[8,128]{1,0:T(8,128)S(1)}, f32[8,128]{1,0:T(8,128)S(1)}, u32[]{:S(2)}, u32[]{:S(2)}) %collective-permute-start.6) | collective-permute-done | bytes 4128 | tf_op jit(solution)/shard_map/ppermute | solution.py:250
  30.4 1.5 %collective-permute-start.7 = (f32[8,128]{1,0:T(8,128)S(1)}, f32[8,128]{1,0:T(8,128)S(1)}, u32[]{:S(2)}, u32[]{:S(2)}) collective-permute-start(f32[8,128]{1,0:T(8,128)S(1)} %add.18), channel_id=1, source_target_pairs={{0,2},{1,3},{2,0},{3,1},{4,6},{5,7},{6,4},{7,5},{8,10},{9,11},{10,... | collective-permute-start | bytes 12296 | tf_op jit(solution)/shard_map/ppermute | solution.py:250
  31.9 2.1 %collective-permute-done.7 = f32[8,128]{1,0:T(8,128)S(1)} collective-permute-done((f32[8,128]{1,0:T(8,128)S(1)}, f32[8,128]{1,0:T(8,128)S(1)}, u32[]{:S(2)}, u32[]{:S(2)}) %collective-permute-start.7) | collective-permute-done | bytes 4128 | tf_op jit(solution)/shard_map/ppermute | solution.py:250
  34.1 2.3 %collective-permute-start.8 = (f32[2,128]{1,0:T(2,128)S(1)}, f32[2,128]{1,0:T(2,128)S(1)}, u32[]{:S(2)}, u32[]{:S(2)}) collective-permute-start(f32[2,128]{1,0:T(2,128)S(1)} %bitcast.6), channel_id=1, source_target_pairs={{0,16},{1,24},{2,0},{3,8},{4,20},{5,28},{6,4},{7,12},{8,17},{9,25}... | collective-permute-start | bytes 3080 | tf_op jit(solution)/shard_map/ppermute | solution.py:279
  36.4 1.3 %collective-permute-done.8 = f32[2,128]{1,0:T(2,128)S(1)} collective-permute-done((f32[2,128]{1,0:T(2,128)S(1)}, f32[2,128]{1,0:T(2,128)S(1)}, u32[]{:S(2)}, u32[]{:S(2)}) %collective-permute-start.8) | collective-permute-done | bytes 1056 | tf_op jit(solution)/shard_map/ppermute | solution.py:279
  37.7 0.6 %copy.7 = f32[2,128]{1,0:T(2,128)} copy(f32[2,128]{1,0:T(2,128)S(1)} %collective-permute-done.8) | data formatting | bytes 2048
  (6 shorter events, 0.0 us)
Async XLA Ops:
  0.0 27.8 %collective-permute-start.3 = (bf16[64,4096]{1,0:T(8,128)(2,1)}, bf16[64,4096]{1,0:T(8,128)(2,1)S(1)}, u32[]{:S(2)}, u32[]{:S(2)}) collective-permute-start(bf16[64,4096]{1,0:T(8,128)(2,1)} %bitcast.3), channel_id=1, source_target_pairs={{0,4},{4,0},{8,12},{12,8},{16,20},{20,16},{24,28},{28,24},{1,5},{5... | collective-permute-start | bytes 1572872 | tf_op jit(solution)/shard_map/ppermute | solution.py:250
  8.9 18.9 %copy-start = (bf16[1,64,4096]{2,1,0:T(8,128)(2,1)S(1)}, bf16[1,64,4096]{2,1,0:T(8,128)(2,1)}, u32[]{:S(2)}) copy-start(bf16[1,64,4096]{2,1,0:T(8,128)(2,1)} %param.9) | copy-start | bytes 1572868
  8.9 6.9 %collective-permute-start = (f32[64,128]{1,0:T(8,128)S(1)}, f32[64,128]{1,0:T(8,128)S(1)}, u32[]{:S(2)}, u32[]{:S(2)}) collective-permute-start(f32[64,128]{1,0:T(8,128)S(1)} %get-tuple-element.7), channel_id=1, source_target_pairs={{0,4},{4,0},{8,12},{12,8},{16,20},{20,16},{24,28},{28,24},{1,5},{5... | collective-permute-start | bytes 98312 | tf_op jit(solution)/shard_map/ppermute | solution.py:250
  15.8 3.9 %collective-permute-start.1 = (f32[64,128]{1,0:T(8,128)S(1)}, f32[64,128]{1,0:T(8,128)S(1)}, u32[]{:S(2)}, u32[]{:S(2)}) collective-permute-start(f32[64,128]{1,0:T(8,128)S(1)} %add.16), channel_id=1, source_target_pairs={{0,8},{4,12},{8,0},{12,4},{16,24},{20,28},{24,16},{28,20},{1,9},{5... | collective-permute-start | bytes 98312 | tf_op jit(solution)/shard_map/ppermute | solution.py:250
  17.6 4.9 %collective-permute-start.4 = (f32[64,128]{1,0:T(8,128)S(1)}, f32[64,128]{1,0:T(8,128)S(1)}, u32[]{:S(2)}, u32[]{:S(2)}) collective-permute-start(f32[64,128]{1,0:T(8,128)S(1)} %get-tuple-element.8.refs_2_), channel_id=1, source_target_pairs={{0,8},{4,12},{8,0},{12,4},{16,24},{20,28},{24,16},{28,20},{1,9},{5... | collective-permute-start | bytes 98312 | tf_op jit(solution)/shard_map/ppermute | solution.py:250
  19.8 5.0 %collective-permute-start.2 = (f32[64,128]{1,0:T(8,128)S(1)}, f32[64,128]{1,0:T(8,128)S(1)}, u32[]{:S(2)}, u32[]{:S(2)}) collective-permute-start(f32[64,128]{1,0:T(8,128)S(1)} %add.17.cov_a), channel_id=1, source_target_pairs={{0,16},{4,20},{8,24},{12,28},{16,0},{20,4},{24,8},{28,12},{1,17},{... | collective-permute-start | bytes 98312 | tf_op jit(solution)/shard_map/ppermute | solution.py:250
  22.6 5.2 %collective-permute-start.5 = (f32[128,128]{1,0:T(8,128)S(1)}, f32[128,128]{1,0:T(8,128)S(1)}, u32[]{:S(2)}, u32[]{:S(2)}) collective-permute-start(f32[128,128]{1,0:T(8,128)S(1)} %pad_maximum_fusion), channel_id=1, source_target_pairs={{0,16},{4,20},{8,24},{12,28},{16,0},{20,4},{24,8},{28,12},{1,17},{... | collective-permute-start | bytes 196616 | tf_op jit(solution)/shard_map/ppermute | solution.py:250
  29.2 1.2 %collective-permute-start.6 = (f32[8,128]{1,0:T(8,128)S(1)}, f32[8,128]{1,0:T(8,128)S(1)}, u32[]{:S(2)}, u32[]{:S(2)}) collective-permute-start(f32[8,128]{1,0:T(8,128)S(1)} %scores.1), channel_id=1, source_target_pairs={{0,1},{1,0},{2,3},{3,2},{4,5},{5,4},{6,7},{7,6},{8,9},{9,8},{10,11... | collective-permute-start | bytes 12296 | tf_op jit(solution)/shard_map/ppermute | solution.py:250
  30.4 3.6 %collective-permute-start.7 = (f32[8,128]{1,0:T(8,128)S(1)}, f32[8,128]{1,0:T(8,128)S(1)}, u32[]{:S(2)}, u32[]{:S(2)}) collective-permute-start(f32[8,128]{1,0:T(8,128)S(1)} %add.18), channel_id=1, source_target_pairs={{0,2},{1,3},{2,0},{3,1},{4,6},{5,7},{6,4},{7,5},{8,10},{9,11},{10,... | collective-permute-start | bytes 12296 | tf_op jit(solution)/shard_map/ppermute | solution.py:250
  34.1 3.6 %collective-permute-start.8 = (f32[2,128]{1,0:T(2,128)S(1)}, f32[2,128]{1,0:T(2,128)S(1)}, u32[]{:S(2)}, u32[]{:S(2)}) collective-permute-start(f32[2,128]{1,0:T(2,128)S(1)} %bitcast.6), channel_id=1, source_target_pairs={{0,16},{1,24},{2,0},{3,8},{4,20},{5,28},{6,4},{7,12},{8,17},{9,25}... | collective-permute-start | bytes 3080 | tf_op jit(solution)/shard_map/ppermute | solution.py:279

commit v2 on v1

--- a/solution.py
+++ b/solution.py
@@ -181,23 +181,17 @@
     )(cov_a, cov_b)
 
 
-def score_kernel(r, scale, inv, *refs):
-    queries, (*grads, out, cond_s, q_v, sems) = refs[:r], refs[r:]
+def score_kernel(r, order, scale, inv, *refs):
+    queries, (*grads, out, cond_s) = refs[:r], refs[r:]
     size = inv.shape[1]
     rank = size // 2
     count = queries[0].shape[0]
-    mine = lax.rem(lax.axis_index("dp"), r)
-    copies = []
-    for k in range(r):
-        at = pl.multiple_of((mine ^ k) * count, count)
-        copy = pltpu.make_async_copy(queries[k], q_v.at[pl.ds(at, count)], sems.at[k])
-        copy.start()
-        copies.append(copy)
     f_out = inv[:rank, :rank]
     f_in = inv[rank:, :]
     twice_in = jnp.concatenate([pltpu.roll(f_in, rank, 1), f_in], axis=0)
-    pieces = [g[at : at + rank, :] for g in grads for at in range(0, g.shape[0], rank)]
-    blocks = len(pieces)
+    came = [(g, at) for g in grads for at in range(0, g.shape[0], rank)]
+    blocks = len(came)
+    pieces = [g[at : at + rank, :] for g, at in (came[order.index(k)] for k in range(blocks))]
     left = dot(f_out, jnp.concatenate(pieces, axis=1), HIGHEST)
     left = jnp.concatenate([left[:, size * k : size * (k + 1)] for k in range(blocks)], axis=0)
     cond = dot(left, twice_in, HIGHEST)
@@ -212,26 +206,28 @@
         odd = cond_s[pl.ds(n + 2 * j + 1, 2 * blocks, stride=rank), :]
         parts.append(jnp.where(low, even, odd))
     flat = jnp.concatenate(parts, axis=1).astype(jnp.bfloat16)
-    for copy in copies:
-        copy.wait()
-    out[...] = dot_t(flat, q_v[...]) * scale
-
-
-def scores_of(r, scale, inv, queries, grads):
+    held = jnp.concatenate([q[...] for q in queries], axis=0)
+    scores = dot_t(flat, held) * scale
+    mine = lax.rem(lax.axis_index("dp"), r)
+    for k in bits(r):
+        turned = jnp.concatenate(
+            [scores[:, (c ^ k) * count : ((c ^ k) + 1) * count] for c in range(r)], axis=1
+        )
+        scores = jnp.where((mine & k) != 0, turned, scores)
+    out[...] = scores
+
+
+def scores_of(r, order, scale, inv, queries, grads):
     size = inv.shape[1]
     blocks = sum(g.shape[0] for g in grads) // (size // 2)
     count, width = queries[0].shape
     return pl.pallas_call(
-        functools.partial(score_kernel, r, scale),
+        functools.partial(score_kernel, r, order, scale),
         name="scores",
         out_shape=jax.ShapeDtypeStruct((2 * blocks, r * count), jnp.float32),
-        in_specs=[VMEM] + [ANY] * r + [VMEM] * len(grads),
+        in_specs=[VMEM] * (1 + r + len(grads)),
         out_specs=VMEM,
-        scratch_shapes=[
-            pltpu.VMEM((3 * blocks * (size // 2), size), jnp.float32),
-            pltpu.VMEM((r * count, width), queries[0].dtype),
-            pltpu.SemaphoreType.DMA((r,)),
-        ],
+        scratch_shapes=[pltpu.VMEM((3 * blocks * (size // 2), size), jnp.float32)],
         compiler_params=pltpu.CompilerParams(vmem_limit_bytes=SMALL_VMEM),
         cost_estimate=pl.CostEstimate(
             flops=4 * blocks * r * count * width,
@@ -250,22 +246,23 @@
         return lax.ppermute(x, axis, [(i, i ^ k) for i in range(n)])
 
     cov, grad = project(acts, grads, proj_in, proj_out)
-    steps = bits(r) + [r * k for k in bits(n_layer)]
+    steps = bits(r) + [r * k for k in reversed(bits(n_layer))]
     queries = [query_grads[0]]
     for k in range(1, r):
         queries.append(swap(query_grads[0], "dp", n_dp, k))
-    gathered = [grad]
+    gathered, order = [grad], [0]
     for s, k in enumerate(steps):
         other = swap(cov, "dp", n_dp, k)
         if k >= r:
             whole = jnp.concatenate(gathered, axis=0) if len(gathered) > 1 else gathered[0]
             gathered.append(swap(whole, "dp", n_dp, k))
+            order += [o ^ (k // r) for o in order]
         if s < len(steps) - 1:
             cov = cov + other
     width = query_grads.shape[2]
     scale = 1.0 / math.sqrt(width * acts.shape[0] * n_layer * length)
     inv = inverses_of(examples * length * n_dp, cov, other)
-    part = scores_of(r, scale, inv, queries, gathered)
+    part = scores_of(r, order, scale, inv, queries, gathered)
     for k in bits(n_layer):
         part = part + swap(part, "layer", n_layer, k)
     half = n_layer // 2

time: 38.7 us -> 38.8 us (level)
  transfers between devices with their start and end apart: 9 -> 9, of which waited for: 7 -> 6; matrix products, arithmetic and copies ran while one was open for 0% -> 0% of each run, Pallas kernels for 22% -> 22%
where the time goes in v2:
time: 38.8 us; the launch traced here: 38.1 us
  waiting for transfers between devices  14.3 us (37%)
  starting transfers between devices  13.4 us (35%)
  Pallas kernels  9.72 us (25%)
  local copies, waits for them, and re-layouts  0.58 us (1%)
    ppermute x8, waiting for transfers between devices, swap(): return lax.ppermute(x, axis, [(i, i ^ k) for i in range(n)])  13 us
    ppermute x8, starting transfers between devices, swap(): return lax.ppermute(x, axis, [(i, i ^ k) for i in range(n)])  10.9 us
    pallas_call x1, Pallas kernels, project(): pl.pallas_call(functools.partial(project_kernel, chunks, 4), name='projec...  5.92 us
    pallas_call x1, Pallas kernels, inverses_of(): pl.pallas_call(functools.partial(inverse_kernel, float(tokens)), name='in...  2.64 us
    ppermute x1, starting transfers between devices, local(): return lax.ppermute(part, ('dp', 'layer'), moves)  2.52 us
    ppermute x1, waiting for transfers between devices, local(): return lax.ppermute(part, ('dp', 'layer'), moves)  1.3 us
    pallas_call x1, Pallas kernels, scores_of(): pl.pallas_call(functools.partial(score_kernel, r, order, scale), name='sc...  1.16 us
  transfers between devices with their start and end apart: 9, of which 6 were waited for; matrix products, arithmetic and copies ran while one was open for 0% of the time, Pallas kernels for 22%

profile of v2, /device:TPU:0, one launch (start us, length us, event | category | flops | bytes accessed | tf_op | source)
XLA Modules:
  0.0 38.1 jit_solution(14853638219422335263)
XLA Ops:
  0.0 3.0 %collective-permute-start.3 = (bf16[64,4096]{1,0:T(8,128)(2,1)}, bf16[64,4096]{1,0:T(8,128)(2,1)S(1)}, u32[]{:S(2)}, u32[]{:S(2)}) collective-permute-start(bf16[64,4096]{1,0:T(8,128)(2,1)} %bitcast.3), channel_id=1, source_target_pairs={{0,4},{4,0},{8,12},{12,8},{16,20},{20,16},{24,28},{28,24},{1,5},{5... | collective-permute-start | bytes 1572872 | tf_op jit(solution)/shard_map/ppermute | solution.py:246
  3.0 5.9 %project.1 = (f32[64,128]{1,0:T(8,128)S(1)}, f32[64,128]{1,0:T(8,128)S(1)}) custom-call(bf16[1,2,128,4096]{3,2,1,0:T(8,128)(2,1)} %acts.1, bf16[1,2,128,14336]{3,2,1,0:T(8,128)(2,1)} %grads.1, bf16[1,64,4096]{2,1,0:T(8,128)(2,1)} %p_in.1, bf16[1,64,14336]{2,1,0:T(8,128)(2,1)} %p_out.1), custom_call_target="tpu_custom_call" | custom-call | flops 603979776 | bytes 11796480 | tf_op jit(solution)/shard_map/project/pallas_call | solution.py:94
  8.9 0.0 copy-start
  8.9 0.1 collective-permute-start
  9.0 6.8 %collective-permute-done = f32[64,128]{1,0:T(8,128)S(1)} collective-permute-done((f32[64,128]{1,0:T(8,128)S(1)}, f32[64,128]{1,0:T(8,128)S(1)}, u32[]{:S(2)}, u32[]{:S(2)}) %collective-permute-start) | collective-permute-done | bytes 32800 | tf_op jit(solution)/shard_map/ppermute | solution.py:246
  15.8 2.8 %collective-permute-start.1 = (f32[64,128]{1,0:T(8,128)S(1)}, f32[64,128]{1,0:T(8,128)S(1)}, u32[]{:S(2)}, u32[]{:S(2)}) collective-permute-start(f32[64,128]{1,0:T(8,128)S(1)} %add.16), channel_id=1, source_target_pairs={{0,16},{4,20},{8,24},{12,28},{16,0},{20,4},{24,8},{28,12},{1,17},{... | collective-permute-start | bytes 98312 | tf_op jit(solution)/shard_map/ppermute | solution.py:246
  18.6 0.1 collective-permute-start.4
  18.8 1.9 %collective-permute-done.1 = f32[64,128]{1,0:T(8,128)S(1)} collective-permute-done((f32[64,128]{1,0:T(8,128)S(1)}, f32[64,128]{1,0:T(8,128)S(1)}, u32[]{:S(2)}, u32[]{:S(2)}) %collective-permute-start.1) | collective-permute-done | bytes 32800 | tf_op jit(solution)/shard_map/ppermute | solution.py:246
  20.7 1.8 %collective-permute-start.2 = (f32[64,128]{1,0:T(8,128)S(1)}, f32[64,128]{1,0:T(8,128)S(1)}, u32[]{:S(2)}, u32[]{:S(2)}) collective-permute-start(f32[64,128]{1,0:T(8,128)S(1)} %add.17.cov_a), channel_id=1, source_target_pairs={{0,8},{4,12},{8,0},{12,4},{16,24},{20,28},{24,16},{28,20},{1,9},{5... | collective-permute-start | bytes 98312 | tf_op jit(solution)/shard_map/ppermute | solution.py:246
  22.5 1.0 %collective-permute-done.4.refs_3_ = f32[64,128]{1,0:T(8,128)S(1)} collective-permute-done((f32[64,128]{1,0:T(8,128)S(1)}, f32[64,128]{1,0:T(8,128)S(1)}, u32[]{:S(2)}, u32[]{:S(2)}) %collective-permute-start.4) | collective-permute-done | bytes 32800 | tf_op jit(solution)/shard_map/ppermute | solution.py:246
  23.5 1.6 %collective-permute-start.5 = (f32[128,128]{1,0:T(8,128)S(1)}, f32[128,128]{1,0:T(8,128)S(1)}, u32[]{:S(2)}, u32[]{:S(2)}) collective-permute-start(f32[128,128]{1,0:T(8,128)S(1)} %pad_maximum_fusion), channel_id=1, source_target_pairs={{0,8},{4,12},{8,0},{12,4},{16,24},{20,28},{24,16},{28,20},{1,9},{5... | collective-permute-start | bytes 196616 | tf_op jit(solution)/shard_map/ppermute | solution.py:246
  25.0 0.0 collective-permute-done.2.cov_b
  25.0 2.6 %inverses.1.inv = f32[128,128]{1,0:T(8,128)S(1)} custom-call(f32[64,128]{1,0:T(8,128)S(1)} %add.17.cov_a, f32[64,128]{1,0:T(8,128)S(1)} %collective-permute-done.2.cov_b), custom_call_target="tpu_custom_call" | custom-call | flops 419430400 | bytes 262144 | tf_op jit(solution)/shard_map/inverses/pallas_call | solution.py:171
  27.7 0.0 collective-permute-done.5.refs_4_
  27.7 0.0 collective-permute-done.3.refs_1_
  27.7 0.0 copy-done
  27.7 1.2 %scores.1 = f32[8,128]{1,0:T(8,128)S(1)} custom-call(f32[128,128]{1,0:T(8,128)S(1)} %inverses.1.inv, bf16[64,4096]{1,0:T(8,128)(2,1)S(1)} %bitcast.4, bf16[64,4096]{1,0:T(8,128)(2,1)S(1)} %collective-permute-done.3.refs_1_, f32[64,128]{1,0:T(8,128)S(1)} %get-tuple-element.8.refs_2_, f32[64,128]{1,0:T(8,128)S(1)} %collective-permute-done.4.refs_3_, ...), custom_call_target="tpu_custom_call" | custom-call | flops 8388608 | bytes 1048576 | tf_op jit(solution)/shard_map/scores/pallas_call | solution.py:224
  28.9 0.0 collective-permute-start.6
  28.9 1.2 %collective-permute-done.6 = f32[8,128]{1,0:T(8,128)S(1)} collective-permute-done((f32[8,128]{1,0:T(8,128)S(1)}, f32[8,128]{1,0:T(8,128)S(1)}, u32[]{:S(2)}, u32[]{:S(2)}) %collective-permute-start.6) | collective-permute-done | bytes 4128 | tf_op jit(solution)/shard_map/ppermute | solution.py:246
  30.1 1.5 %collective-permute-start.7 = (f32[8,128]{1,0:T(8,128)S(1)}, f32[8,128]{1,0:T(8,128)S(1)}, u32[]{:S(2)}, u32[]{:S(2)}) collective-permute-start(f32[8,128]{1,0:T(8,128)S(1)} %add.18), channel_id=1, source_target_pairs={{0,2},{1,3},{2,0},{3,1},{4,6},{5,7},{6,4},{7,5},{8,10},{9,11},{10,... | collective-permute-start | bytes 12296 | tf_op jit(solution)/shard_map/ppermute | solution.py:246
  31.6 2.1 %collective-permute-done.7 = f32[8,128]{1,0:T(8,128)S(1)} collective-permute-done((f32[8,128]{1,0:T(8,128)S(1)}, f32[8,128]{1,0:T(8,128)S(1)}, u32[]{:S(2)}, u32[]{:S(2)}) %collective-permute-start.7) | collective-permute-done | bytes 4128 | tf_op jit(solution)/shard_map/ppermute | solution.py:246
  33.7 2.5 %collective-permute-start.8 = (f32[2,128]{1,0:T(2,128)S(1)}, f32[2,128]{1,0:T(2,128)S(1)}, u32[]{:S(2)}, u32[]{:S(2)}) collective-permute-start(f32[2,128]{1,0:T(2,128)S(1)} %bitcast.6), channel_id=1, source_target_pairs={{0,16},{1,24},{2,0},{3,8},{4,20},{5,28},{6,4},{7,12},{8,17},{9,25}... | collective-permute-start | bytes 3080 | tf_op jit(solution)/shard_map/ppermute | solution.py:276
  36.2 1.3 %collective-permute-done.8 = f32[2,128]{1,0:T(2,128)S(1)} collective-permute-done((f32[2,128]{1,0:T(2,128)S(1)}, f32[2,128]{1,0:T(2,128)S(1)}, u32[]{:S(2)}, u32[]{:S(2)}) %collective-permute-start.8) | collective-permute-done | bytes 1056 | tf_op jit(solution)/shard_map/ppermute | solution.py:276
  37.5 0.6 %copy.7 = f32[2,128]{1,0:T(2,128)} copy(f32[2,128]{1,0:T(2,128)S(1)} %collective-permute-done.8) | data formatting | bytes 2048
  (6 shorter events, 0.0 us)
Async XLA Ops:
  0.0 27.7 %collective-permute-start.3 = (bf16[64,4096]{1,0:T(8,128)(2,1)}, bf16[64,4096]{1,0:T(8,128)(2,1)S(1)}, u32[]{:S(2)}, u32[]{:S(2)}) collective-permute-start(bf16[64,4096]{1,0:T(8,128)(2,1)} %bitcast.3), channel_id=1, source_target_pairs={{0,4},{4,0},{8,12},{12,8},{16,20},{20,16},{24,28},{28,24},{1,5},{5... | collective-permute-start | bytes 1572872 | tf_op jit(solution)/shard_map/ppermute | solution.py:246
  8.9 18.8 %copy-start = (bf16[1,64,4096]{2,1,0:T(8,128)(2,1)S(1)}, bf16[1,64,4096]{2,1,0:T(8,128)(2,1)}, u32[]{:S(2)}) copy-start(bf16[1,64,4096]{2,1,0:T(8,128)(2,1)} %param.9) | copy-start | bytes 1572868
  8.9 6.9 %collective-permute-start = (f32[64,128]{1,0:T(8,128)S(1)}, f32[64,128]{1,0:T(8,128)S(1)}, u32[]{:S(2)}, u32[]{:S(2)}) collective-permute-start(f32[64,128]{1,0:T(8,128)S(1)} %get-tuple-element.7), channel_id=1, source_target_pairs={{0,4},{4,0},{8,12},{12,8},{16,20},{20,16},{24,28},{28,24},{1,5},{5... | collective-permute-start | bytes 98312 | tf_op jit(solution)/shard_map/ppermute | solution.py:246
  15.8 4.8 %collective-permute-start.1 = (f32[64,128]{1,0:T(8,128)S(1)}, f32[64,128]{1,0:T(8,128)S(1)}, u32[]{:S(2)}, u32[]{:S(2)}) collective-permute-start(f32[64,128]{1,0:T(8,128)S(1)} %add.16), channel_id=1, source_target_pairs={{0,16},{4,20},{8,24},{12,28},{16,0},{20,4},{24,8},{28,12},{1,17},{... | collective-permute-start | bytes 98312 | tf_op jit(solution)/shard_map/ppermute | solution.py:246
  18.6 4.8 %collective-permute-start.4 = (f32[64,128]{1,0:T(8,128)S(1)}, f32[64,128]{1,0:T(8,128)S(1)}, u32[]{:S(2)}, u32[]{:S(2)}) collective-permute-start(f32[64,128]{1,0:T(8,128)S(1)} %get-tuple-element.8.refs_2_), channel_id=1, source_target_pairs={{0,16},{4,20},{8,24},{12,28},{16,0},{20,4},{24,8},{28,12},{1,17},{... | collective-permute-start | bytes 98312 | tf_op jit(solution)/shard_map/ppermute | solution.py:246
  20.7 4.4 %collective-permute-start.2 = (f32[64,128]{1,0:T(8,128)S(1)}, f32[64,128]{1,0:T(8,128)S(1)}, u32[]{:S(2)}, u32[]{:S(2)}) collective-permute-start(f32[64,128]{1,0:T(8,128)S(1)} %add.17.cov_a), channel_id=1, source_target_pairs={{0,8},{4,12},{8,0},{12,4},{16,24},{20,28},{24,16},{28,20},{1,9},{5... | collective-permute-start | bytes 98312 | tf_op jit(solution)/shard_map/ppermute | solution.py:246
  23.5 4.3 %collective-permute-start.5 = (f32[128,128]{1,0:T(8,128)S(1)}, f32[128,128]{1,0:T(8,128)S(1)}, u32[]{:S(2)}, u32[]{:S(2)}) collective-permute-start(f32[128,128]{1,0:T(8,128)S(1)} %pad_maximum_fusion), channel_id=1, source_target_pairs={{0,8},{4,12},{8,0},{12,4},{16,24},{20,28},{24,16},{28,20},{1,9},{5... | collective-permute-start | bytes 196616 | tf_op jit(solution)/shard_map/ppermute | solution.py:246
  28.9 1.2 %collective-permute-start.6 = (f32[8,128]{1,0:T(8,128)S(1)}, f32[8,128]{1,0:T(8,128)S(1)}, u32[]{:S(2)}, u32[]{:S(2)}) collective-permute-start(f32[8,128]{1,0:T(8,128)S(1)} %scores.1), channel_id=1, source_target_pairs={{0,1},{1,0},{2,3},{3,2},{4,5},{5,4},{6,7},{7,6},{8,9},{9,8},{10,11... | collective-permute-start | bytes 12296 | tf_op jit(solution)/shard_map/ppermute | solution.py:246
  30.1 3.6 %collective-permute-start.7 = (f32[8,128]{1,0:T(8,128)S(1)}, f32[8,128]{1,0:T(8,128)S(1)}, u32[]{:S(2)}, u32[]{:S(2)}) collective-permute-start(f32[8,128]{1,0:T(8,128)S(1)} %add.18), channel_id=1, source_target_pairs={{0,2},{1,3},{2,0},{3,1},{4,6},{5,7},{6,4},{7,5},{8,10},{9,11},{10,... | collective-permute-start | bytes 12296 | tf_op jit(solution)/shard_map/ppermute | solution.py:246
  33.7 3.8 %collective-permute-start.8 = (f32[2,128]{1,0:T(2,128)S(1)}, f32[2,128]{1,0:T(2,128)S(1)}, u32[]{:S(2)}, u32[]{:S(2)}) collective-permute-start(f32[2,128]{1,0:T(2,128)S(1)} %bitcast.6), channel_id=1, source_target_pairs={{0,16},{1,24},{2,0},{3,8},{4,20},{5,28},{6,4},{7,12},{8,17},{9,25}... | collective-permute-start | bytes 3080 | tf_op jit(solution)/shard_map/ppermute | solution.py:276
